TPU v7x, 256 devices: a whole 4x4x8 slice. The times are simulated.
256 devices in a mesh: ctx: 32 (over x_lo, z, core), exp: 8 (over x_hi, y).
Axes of the slice: x: 4 (x_hi: 2, x_lo: 2; x = x_hi * 2 + x_lo), y: 4, z: 8, core: 2. Of those that a mesh axis runs over, the one named last changes fastest.
Arguments:
- queries: bfloat16 [8192, 8192], P('ctx', 'exp'), may hold values from -8 to 8
- keys: bfloat16 [8192, 512], P('ctx'), may hold values from -4 to 4
- values: bfloat16 [8192, 512], P('ctx'), may hold values from -6 to 6
- w_out: bfloat16 [8192, 4096], P('exp'), may hold values from -0.5 to 0.5
- residual: bfloat16 [8192, 4096], P(('ctx', 'exp')), may hold values from -1.5 to 1.5
- norm_gain: bfloat16 [4096], replicated, may hold values from 0.099609375 to 1.8984375
- expert_ids: int32 [8192, 2], P(('ctx', 'exp')), may hold values from 0 to 7, all different within a row; in each aligned block of 32 rows (0 to 31, 32 to 63, ...) at most 16 rows name the same one
- gate_weights: float32 [8192, 2], P(('ctx', 'exp')), may hold values from 0.2 to 1
- w_gate: bfloat16 [8, 4096, 768], P('exp', 'ctx'), may hold values from -0.09375 to 0.09375
- w_up: bfloat16 [8, 4096, 768], P('exp', 'ctx'), may hold values from -0.09375 to 0.09375
- w_down: bfloat16 [8, 768, 4096], P('exp', None, 'ctx'), may hold values from -0.21875 to 0.21875
Outputs:
- layer_out: bfloat16 [8192, 4096], P(('ctx', 'exp'))
Inputs may be any that keep to these rules, and one draw needn't show every extreme that they name: `expert_ids`: each row names 2 different experts; within each aligned block of 32 rows (the rows of one device) no expert is named by more than 16 rows.
All inputs are finite; a program needn't handle non-finite values.
Results may differ from a plain program's by a relative error of at most 0.025.
Values may be sent and summed in bfloat16 or wider, within the bound.
A program may use at most 128 MiB of HBM per device.

v0:
```python
import math
import jax
import jax.numpy as jnp
from jax import lax
from jax.sharding import PartitionSpec as P

D = 4096
HQ = 64
KVH = 4
HD = 128


def body(
    queries,
    keys,
    values,
    w_out,
    residual,
    norm_gain,
    expert_ids,
    gate_weights,
    w_gate,
    w_up,
    w_down,
):
    tok_rows = queries.shape[0]
    half_rows = tok_rows // 2
    exp_count = lax.axis_size("exp")
    heads_here = HQ // exp_count
    group = HQ // KVH
    kv_here = max(1, heads_here // group)
    heads_per_kv = heads_here // kv_here
    exp_index = lax.axis_index("exp")
    ctx_index = lax.axis_index("ctx")
    kv_first = exp_index * heads_here // group
    key_cols = lax.dynamic_slice_in_dim(keys, kv_first * HD, kv_here * HD, 1)
    value_cols = lax.dynamic_slice_in_dim(values, kv_first * HD, kv_here * HD, 1)
    scale = 1.0 / math.sqrt(HD)
    first_rows = queries[:half_rows]
    second_rows = queries[half_rows:]
    first_start = ctx_index * tok_rows
    second_start = ctx_index * tok_rows + half_rows
    query_sets = (
        first_rows.reshape(half_rows, kv_here, heads_per_kv, HD),
        second_rows.reshape(half_rows, kv_here, heads_per_kv, HD),
    )
    query_positions = (
        first_start + jnp.arange(half_rows, dtype=jnp.int32),
        second_start + jnp.arange(half_rows, dtype=jnp.int32),
    )
    last_positions = (first_start + half_rows - 1, second_start + half_rows - 1)

    def block_update(carry, query_four, query_pos, key_block, value_block, key_start):
        run_max, run_sum, run_acc = carry
        width = key_block.shape[0]
        key_three = key_block.reshape(width, kv_here, HD)
        value_three = value_block.reshape(width, kv_here, HD)
        scores = (
            jnp.einsum("tghd,kgd->ghtk", query_four, key_three, preferred_element_type=jnp.float32)
            * scale
        )
        key_pos = key_start + jnp.arange(width, dtype=jnp.int32)
        allowed = key_pos[None, :] <= query_pos[:, None]
        scores = jnp.where(allowed, scores, -1e30)
        new_max = jnp.maximum(run_max, jnp.max(scores, axis=-1))
        probs = jnp.where(allowed, jnp.exp(scores - new_max[..., None]), 0.0)
        factor = jnp.exp(run_max - new_max)
        run_sum = run_sum * factor + jnp.sum(probs, axis=-1)
        weighted = jnp.einsum(
            "ghtk,kgd->ghtd",
            probs.astype(jnp.bfloat16),
            value_three,
            preferred_element_type=jnp.float32,
        )
        run_acc = run_acc * factor[..., None] + weighted
        return (new_max, run_sum, run_acc)

    start_max = jnp.full((kv_here, heads_per_kv, half_rows), -1e30, jnp.float32)
    start_sum = jnp.zeros((kv_here, heads_per_kv, half_rows), jnp.float32)
    start_acc = jnp.zeros((kv_here, heads_per_kv, half_rows, HD), jnp.float32)
    start_state = (start_max, start_sum, start_acc)
    key_piece = lax.all_gather(key_cols, "ctx", axis=0, tiled=True)
    value_piece = lax.all_gather(value_cols, "ctx", axis=0, tiled=True)
    count = key_piece.shape[0]
    width = 512

    def one_block(index, inner):
        key_start = index * width
        key_block = lax.dynamic_slice_in_dim(key_piece, key_start, width, 0)
        value_block = lax.dynamic_slice_in_dim(value_piece, key_start, width, 0)
        updated = []
        for which in range(2):
            query_four = query_sets[which]
            query_pos = query_positions[which]
            updated.append(
                lax.cond(
                    key_start > last_positions[which],
                    lambda state: state,
                    lambda state: block_update(
                        state, query_four, query_pos, key_block, value_block, key_start
                    ),
                    inner[which],
                )
            )
        return (updated[0], updated[1])

    states = lax.fori_loop(0, count // width, one_block, (start_state, start_state))
    halves = []
    for which in range(2):
        run_max, run_sum, run_acc = states[which]
        halves.append(
            jnp.transpose(run_acc / run_sum[..., None], (2, 0, 1, 3))
            .reshape(half_rows, heads_here * HD)
            .astype(jnp.bfloat16)
        )
    attn_second = halves[1]
    attn = jnp.concatenate([halves[0], attn_second], axis=0)
    projected = lax.psum_scatter(
        jnp.dot(attn, w_out, preferred_element_type=jnp.float32).astype(jnp.bfloat16),
        "exp",
        scatter_dimension=0,
        tiled=True,
    ).astype(jnp.float32)
    hidden_state = (residual.astype(jnp.float32) + projected).astype(jnp.bfloat16)
    state_f = hidden_state.astype(jnp.float32)
    inv_rms = 1.0 / jnp.sqrt(jnp.mean(state_f * state_f, axis=1, keepdims=True) + 1e-06)
    normed = (state_f * inv_rms * norm_gain.astype(jnp.float32)[None, :]).astype(jnp.bfloat16)
    rows_here = expert_ids.shape[0]
    top_count = expert_ids.shape[1]
    experts_all = w_gate.shape[0] * exp_count
    capacity = min(rows_here, 2 * rows_here * top_count // experts_all)
    flat_ids = expert_ids.reshape(-1)
    onehot = (flat_ids[:, None] == jnp.arange(experts_all, dtype=jnp.int32)[None, :]).astype(
        jnp.int32
    )
    earlier = jnp.cumsum(onehot, axis=0) - onehot
    slot_index = jnp.sum(earlier * onehot, axis=1)
    target = flat_ids * capacity + slot_index
    picks = target[:, None] == jnp.arange(experts_all * capacity, dtype=jnp.int32)[None, :]
    dispatch_table = jnp.any(
        picks.reshape(rows_here, top_count, experts_all * capacity), axis=1
    ).astype(jnp.bfloat16)
    outgoing = jnp.einsum(
        "rs,rd->sd", dispatch_table, normed, preferred_element_type=jnp.float32
    ).astype(jnp.bfloat16)
    arrived = lax.all_to_all(
        outgoing.reshape(experts_all, capacity, D), "exp", split_axis=0, concat_axis=0, tiled=True
    )
    slot_rows = arrived.reshape(experts_all * capacity, D)
    gate_local = w_gate[0]
    up_local = w_up[0]
    gate_pre = jnp.dot(
        slot_rows,
        lax.all_gather(gate_local, "ctx", axis=0, tiled=True),
        preferred_element_type=jnp.float32,
    )
    up_pre = jnp.dot(
        slot_rows,
        lax.all_gather(up_local, "ctx", axis=0, tiled=True),
        preferred_element_type=jnp.float32,
    )
    expert_hidden = (jax.nn.silu(gate_pre) * up_pre).astype(jnp.bfloat16)
    down_local = w_down[0]
    expert_result = jnp.dot(
        expert_hidden,
        lax.all_gather(down_local, "ctx", axis=1, tiled=True),
        preferred_element_type=jnp.float32,
    ).astype(jnp.bfloat16)
    returned = lax.all_to_all(
        expert_result.reshape(experts_all, capacity, D),
        "exp",
        split_axis=0,
        concat_axis=0,
        tiled=True,
    )
    returned_flat = returned.reshape(experts_all * capacity, D)
    picked = jnp.dot(picks.astype(jnp.bfloat16), returned_flat, preferred_element_type=jnp.float32)
    weighted = gate_weights[:, :, None] * picked.reshape(rows_here, top_count, D)
    return (state_f + jnp.sum(weighted, axis=1)).astype(jnp.bfloat16)


def solution(mesh):
    placed = (
        P("ctx", "exp"),
        P("ctx", None),
        P("ctx", None),
        P("exp", None),
        P(("ctx", "exp"), None),
        P(),
        P(("ctx", "exp"), None),
        P(("ctx", "exp"), None),
        P("exp", "ctx", None),
        P("exp", "ctx", None),
        P("exp", None, "ctx"),
    )
    return jax.shard_map(
        body, mesh=mesh, in_specs=placed, out_specs=P(("ctx", "exp"), None), check_vma=False
    )
```

profile of v0, /device:TPU:2, one launch (start us, length us, event | category | flops | bytes accessed | tf_op | source)
XLA Modules:
  0.0 573.4 jit_solution(10112256670926563452)
XLA Ops:
  8.2 1.5 constant_dynamic-slice_fusion.3
  9.7 1.1 fusion.83
  11.5 64.9 %all-gather.11.cloned.1.call-done = bf16[8192,128]{1,0:T(8,128)(2,1)} async-done(((bf16[256,128]{1,0:T(8,128)(2,1)}), bf16[8192,128]{1,0:T(8,128)(2,1)}) %all-gather.11.cloned.1.call-update) | async-done | bytes 2097168 | tf_op jit(solution)/shard_map/all_gather | solution.py:83
  76.4 66.3 %all-gather.9.cloned.1.call-done = bf16[8192,128]{1,0:T(8,128)(2,1)} async-done(((bf16[256,128]{1,0:T(8,128)(2,1)}), bf16[8192,128]{1,0:T(8,128)(2,1)}) %all-gather.9.cloned.1.call-update) | async-done | bytes 2097168 | tf_op jit(solution)/shard_map/all_gather | solution.py:82
  142.8 54.4 %while.24 = (s32[]{:T(128)}, f32[1,8,128]{2,1,0:T(8,128)S(1)}, f32[1,8,128]{2,1,0:T(8,128)S(1)}, f32[1,8,128,128]{3,2,1,0:T(8,128)S(1)}, f32[1,8,128]{2,1,0:T(8,...) while((s32[]{:T(128)}, f32[1,8,128]{2,1,0:T(8,128)S(1)}, ...), condition=%wide.region_9.10_spmd.clone, body=%wide.region_0.9_spmd.clone.sunk | while | flops 551165184 | bytes 16921084 | solution.py:107
  142.8 1.0 constant_dynamic-slice_fusion.5
  143.8 2.0 conditional.7
  145.9 2.0 conditional.6
  148.0 1.0 constant_dynamic-slice_fusion.5
  149.0 2.0 conditional.7
  151.1 2.0 conditional.6
  153.1 1.0 constant_dynamic-slice_fusion.5
  154.1 2.0 conditional.7
  156.2 2.0 conditional.6
  158.3 1.0 constant_dynamic-slice_fusion.5
  159.3 2.0 conditional.7
  161.4 2.0 conditional.6
  163.4 1.0 constant_dynamic-slice_fusion.5
  164.5 2.0 conditional.7
  166.5 2.0 conditional.6
  168.6 1.0 constant_dynamic-slice_fusion.5
  169.6 2.0 conditional.7
  171.7 2.0 conditional.6
  173.8 1.0 constant_dynamic-slice_fusion.5
  174.8 2.0 conditional.7
  176.8 2.0 conditional.6
  178.9 1.0 constant_dynamic-slice_fusion.5
  179.9 2.0 conditional.7
  182.0 2.0 conditional.6
  184.1 1.0 constant_dynamic-slice_fusion.5
  185.1 2.0 conditional.7
  187.1 2.0 conditional.6
  189.2 1.0 constant_dynamic-slice_fusion.5
  190.4 1.0 constant_dynamic-slice_fusion.5
  191.5 1.0 constant_dynamic-slice_fusion.5
  192.7 1.0 constant_dynamic-slice_fusion.5
  195.0 1.0 constant_dynamic-slice_fusion.5
  197.8 7.1 %convolution_convert_fusion = bf16[256,4096]{1,0:T(8,128)(2,1)} fusion(bf16[1024,4096]{1,0:T(8,128)(2,1)} %param.20, bf16[128,1024]{0,1:T(8,128)(2,1)S(1)} %bitcast.139, bf16[128,1024]{0,1:T(8,128)(2,1)S(1)} %bitcast.138), kind=kOutput, calls=%fused_computation.64 | convolution fusion | flops 2149580800 | bytes 11010048 | tf_op jit(solution)/shard_map/dot_general | solution.py:119
  207.5 101.7 %reduce-scatter.2.cloned.1.call-done = bf16[32,4096]{1,0:T(8,128)(2,1)} async-done(((bf16[256,4096]{1,0:T(8,128)(2,1)}), bf16[32,4096]{1,0:T(8,128)(2,1)}) %reduce-scatter.2.cloned.1.call-update) | async-done | bytes 262160 | tf_op jit(solution)/shard_map/reduce_scatter | solution.py:118
  309.2 1.1 fusion.60
  310.3 1.5 convolution_convert_fusion.1
  311.8 25.3 %all_to_all.10 = bf16[8,16,4096]{2,1,0:T(8,128)(2,1)S(1)} all-to-all(bf16[8,16,4096]{2,1,0:T(8,128)(2,1)S(1)} %bitcast.130), channel_id=1, replica_groups=mesh['ctx'=32,'exp'=8] {'exp'}, dimensions={0} | all-to-all | bytes 2097152 | tf_op jit(solution)/shard_map/all_to_all | solution.py:146
  337.1 43.7 %all-gather.13.cloned.1.call-done = bf16[1,4096,768]{2,1,0:T(8,128)(2,1)} async-done(((bf16[1,128,768]{2,1,0:T(8,128)(2,1)}), bf16[1,4096,768]{2,1,0:T(8,128)(2,1)}) %all-gather.13.cloned.1.call-update) | async-done | bytes 6291472 | tf_op jit(solution)/shard_map/all_gather | solution.py:154
  380.8 3.8 fusion.46
  384.6 67.9 %all-gather.15.cloned.1.call-done = bf16[1,4096,768]{2,1,0:T(8,128)(2,1)} async-done(((bf16[1,128,768]{2,1,0:T(8,128)(2,1)}), bf16[1,4096,768]{2,1,0:T(8,128)(2,1)}) %all-gather.15.cloned.1.call-update) | async-done | bytes 6291472 | tf_op jit(solution)/shard_map/all_gather | solution.py:159
  452.5 82.3 %all-gather.17.cloned.1.call-done = bf16[1,768,4096]{2,1,0:T(8,128)(2,1)} async-done(((bf16[1,768,128]{2,1,0:T(8,128)(2,1)}), bf16[1,768,4096]{2,1,0:T(8,128)(2,1)}) %all-gather.17.cloned.1.call-update) | async-done | bytes 6291472 | tf_op jit(solution)/shard_map/all_gather | solution.py:166
  534.7 7.1 %fusion.48 = bf16[128,4096]{1,0:T(8,128)(2,1)S(1)} fusion(bf16[1,768,4096]{2,1,0:T(8,128)(2,1)} %all-gather.17.cloned.1.call-done, bf16[128,4096]{1,0:T(8,128)(2,1)S(1)} %bitcast.128, bf16[1,4096,768]{2,1,0:T(8,128)(2,1)} %all-gather.15.cloned.1.call-done, f32[128,768]{1,0:T(8,128)S(1)} %fusion.46), kind=kOutput, calls=%fused_computation.65 | convolution fusion | flops 1611726848 | bytes 15073280 | tf_op jit(solution)/shard_map/dot_general | solution.py:164
  541.8 23.5 %all_to_all.11 = bf16[8,16,4096]{2,1,0:T(8,128)(2,1)S(1)} all-to-all(bf16[8,16,4096]{2,1,0:T(8,128)(2,1)S(1)} %bitcast.129), channel_id=1, replica_groups=mesh['ctx'=32,'exp'=8] {'exp'}, dimensions={0} | all-to-all | bytes 2097152 | tf_op jit(solution)/shard_map/all_to_all | solution.py:169
  (290 shorter events, 44.6 us)
Async XLA Ops:
  6.5 1.0 copy-start
  6.5 69.9 %all-gather.11.cloned.1.call-start = ((), (), s32[]{:S(2)}) async-start(), calls=%async_computation.4 | async-start | bytes 2162688 | tf_op jit(solution)/shard_map/all_gather | solution.py:83
  8.1 134.5 %all-gather.9.cloned.1.call-start = ((), (), s32[]{:S(2)}) async-start(), calls=%async_computation.3 | async-start | bytes 2162688 | tf_op jit(solution)/shard_map/all_gather | solution.py:82
  9.7 299.5 %reduce-scatter.2.cloned.1.call-start = ((), (), s32[]{:S(2)}) async-start(), calls=%async_computation.5 | async-start | bytes 2359296 | tf_op jit(solution)/shard_map/reduce_scatter | solution.py:118
  204.8 1.8 copy-start.4
  204.8 2.5 copy-start.3
  204.8 104.3 %copy-start.1 = (bf16[32,4096]{1,0:T(8,128)(2,1)S(1)}, bf16[32,4096]{1,0:T(8,128)(2,1)}, u32[]{:S(2)}) copy-start(bf16[32,4096]{1,0:T(8,128)(2,1)} %param.21) | copy-start | bytes 786436
  204.9 176.0 %all-gather.13.cloned.1.call-start = ((), (), s32[]{:S(2)}) async-start(), calls=%async_computation.6 | async-start | bytes 6488064 | tf_op jit(solution)/shard_map/all_gather | solution.py:154
  205.4 247.0 %all-gather.15.cloned.1.call-start = ((), (), s32[]{:S(2)}) async-start(), calls=%async_computation.7 | async-start | bytes 6488064 | tf_op jit(solution)/shard_map/all_gather | solution.py:159
  206.0 328.7 %all-gather.17.cloned.1.call-start = ((), (), s32[]{:S(2)}) async-start(), calls=%async_computation.8 | async-start | bytes 6488064 | tf_op jit(solution)/shard_map/all_gather | solution.py:166
  541.8 23.6 %copy-start.5 = (f32[32,2]{0,1:T(2,128)S(1)}, f32[32,2]{0,1:T(2,128)}, u32[]{:S(2)}) copy-start(f32[32,2]{0,1:T(2,128)} %param.24) | copy-start | bytes 772
  541.8 23.9 %copy-start.2 = (bf16[32,4096]{1,0:T(8,128)(2,1)S(1)}, bf16[32,4096]{1,0:T(8,128)(2,1)}, u32[]{:S(2)}) copy-start(bf16[32,4096]{1,0:T(8,128)(2,1)} %reduce-scatter.2.cloned.1.call-done) | copy-start | bytes 786436
Sparse Core Ops, SparseCore 0:
  9.2 67.1 all-gather.10
  78.3 64.3 all-gather.8
  205.0 104.1 reduce-scatter.1
  310.9 69.8 all-gather.12
  382.5 69.9 all-gather.14
  454.1 80.5 all-gather.16
where the time goes:
time: 574 us; the launch traced here: 573 us
  waiting for transfers between devices  428 us (75%)
  blocking collectives  48.9 us (9%)
  matrix products  42.9 us (7%)
  local copies, waits for them, and re-layouts  21.8 us (4%)
  other arithmetic  14.7 us (3%)
  between operations  13.7 us (2%)
    reduce_scatter x1, waiting for transfers between devices, body(): lax.psum_scatter(jnp.dot(attn, w_out, preferred_element_type=jnp.float32)...  102 us
    all_gather x1, waiting for transfers between devices, body(): lax.all_gather(down_local, 'ctx', axis=1, tiled=True)  82.3 us
    all_gather x1, waiting for transfers between devices, body(): lax.all_gather(up_local, 'ctx', axis=0, tiled=True)  67.9 us
    all_gather x1, waiting for transfers between devices, body(): key_piece = lax.all_gather(key_cols, 'ctx', axis=0, tiled=True)  66.3 us
    all_gather x1, waiting for transfers between devices, body(): value_piece = lax.all_gather(value_cols, 'ctx', axis=0, tiled=True)  64.9 us
    all_gather x1, waiting for transfers between devices, body(): lax.all_gather(gate_local, 'ctx', axis=0, tiled=True)  43.7 us
    all_to_all x1, blocking collectives, body(): lax.all_to_all(outgoing.reshape(experts_all, capacity, D), 'exp', split_a...  25.3 us
    all_to_all x1, blocking collectives, body(): lax.all_to_all(expert_result.reshape(experts_all, capacity, D), 'exp', sp...  23.5 us
  transfers between devices with their start and end apart: 6, of which 6 were waited for; matrix products, arithmetic and copies ran while one was open for 2% of the time, Pallas kernels for 0%

commit v1 on v0

--- a/solution.py
+++ b/solution.py
@@ -3,11 +3,18 @@
 import jax.numpy as jnp
 from jax import lax
 from jax.sharding import PartitionSpec as P
+from jax.lax import all_to_all, axis_size
 
 D = 4096
 HQ = 64
 KVH = 4
 HD = 128
+
+
+def supply_all_numbers_on(content):
+    all_values = jnp.stack(axis_size("ctx") * [content])
+    left_arr = all_to_all(all_values, "ctx", 0, 0)
+    return jnp.concatenate(left_arr, axis=1)
 
 
 def body(
@@ -162,9 +169,7 @@
     expert_hidden = (jax.nn.silu(gate_pre) * up_pre).astype(jnp.bfloat16)
     down_local = w_down[0]
     expert_result = jnp.dot(
-        expert_hidden,
-        lax.all_gather(down_local, "ctx", axis=1, tiled=True),
-        preferred_element_type=jnp.float32,
+        expert_hidden, supply_all_numbers_on(down_local), preferred_element_type=jnp.float32
     ).astype(jnp.bfloat16)
     returned = lax.all_to_all(
         expert_result.reshape(experts_all, capacity, D),

time: 574 us -> 583 us (1.016)
  blocking collectives: 48.9 us -> 22.5 us
  waiting for transfers between devices: 428 us -> 448 us
  starting transfers between devices: 0.2 us -> 11.1 us
    all_to_all x0 -> x2, waiting for transfers between devices: none -> 120 us  [the longest x1 97.4 us: supply_all_numbers_on(): left_arr = all_to_all(all_values, 'ctx', 0, 0)]
    all_gather x1 -> x0, waiting for transfers between devices: 82.3 us -> none  [body(): lax.all_gather(down_local, 'ctx', axis=1, tiled=True)]
    all_gather x1, waiting for transfers between devices: 67.9 us -> 21.8 us  [body(): lax.all_gather(up_local, 'ctx', axis=0, tiled=True)]
    all_gather x1, waiting for transfers between devices: 43.7 us -> 71.5 us  [body(): lax.all_gather(gate_local, 'ctx', axis=0, tiled=True)]
    all_to_all x1 -> x0, blocking collectives: 25.3 us -> none  [body(): lax.all_to_all(outgoing.reshape(experts_all, capacity, D), 'exp', split_a...]
    all_to_all x0 -> x2, starting transfers between devices: none -> 10.7 us  [the longest x1 6.16 us: supply_all_numbers_on(): left_arr = all_to_all(all_values, 'ctx', 0, 0)]
  transfers between devices with their start and end apart: 6 -> 7, of which waited for: 6 -> 7; matrix products, arithmetic and copies ran while one was open for 2% -> 3% of each run, Pallas kernels for 0% -> 0%
where the time goes in v1:
time: 583 us; the launch traced here: 582 us
  waiting for transfers between devices  448 us (77%)
  matrix products  44.5 us (8%)
  local copies, waits for them, and re-layouts  25.3 us (4%)
  blocking collectives  22.5 us (4%)
  other arithmetic  14.7 us (3%)
  between operations  13.4 us (2%)
  starting transfers between devices  11.1 us (2%)
    reduce_scatter x1, waiting for transfers between devices, body(): lax.psum_scatter(jnp.dot(attn, w_out, preferred_element_type=jnp.float32)...  103 us
    all_to_all x1, waiting for transfers between devices, supply_all_numbers_on(): left_arr = all_to_all(all_values, 'ctx', 0, 0)  97.4 us
    all_gather x1, waiting for transfers between devices, body(): lax.all_gather(gate_local, 'ctx', axis=0, tiled=True)  71.5 us
    all_gather x1, waiting for transfers between devices, body(): value_piece = lax.all_gather(value_cols, 'ctx', axis=0, tiled=True)  66.3 us
    all_gather x1, waiting for transfers between devices, body(): key_piece = lax.all_gather(key_cols, 'ctx', axis=0, tiled=True)  64.9 us
    all_to_all x1, blocking collectives, body(): lax.all_to_all(expert_result.reshape(experts_all, capacity, D), 'exp', sp...  22.5 us
    all_to_all x1, waiting for transfers between devices, body(): lax.all_to_all(outgoing.reshape(experts_all, capacity, D), 'exp', split_a...  22.4 us
    all_gather x1, waiting for transfers between devices, body(): lax.all_gather(up_local, 'ctx', axis=0, tiled=True)  21.8 us
  transfers between devices with their start and end apart: 7, of which 7 were waited for; matrix products, arithmetic and copies ran while one was open for 3% of the time, Pallas kernels for 0%

profile of v1, /device:TPU:2, one launch (start us, length us, event | category | flops | bytes accessed | tf_op | source)
XLA Modules:
  0.0 582.4 jit_solution(4365203806504898888)
XLA Ops:
  8.2 1.5 constant_dynamic-slice_fusion.2
  9.7 1.1 fusion.78
  11.5 64.9 %all-gather.7.cloned.1.call-done = bf16[8192,128]{1,0:T(8,128)(2,1)} async-done(((bf16[256,128]{1,0:T(8,128)(2,1)}), bf16[8192,128]{1,0:T(8,128)(2,1)}) %all-gather.7.cloned.1.call-update) | async-done | bytes 2097168 | tf_op jit(solution)/shard_map/all_gather | solution.py:89
  76.4 66.3 %all-gather.9.cloned.1.call-done = bf16[8192,128]{1,0:T(8,128)(2,1)} async-done(((bf16[256,128]{1,0:T(8,128)(2,1)}), bf16[8192,128]{1,0:T(8,128)(2,1)}) %all-gather.9.cloned.1.call-update) | async-done | bytes 2097168 | tf_op jit(solution)/shard_map/all_gather | solution.py:90
  142.8 54.4 %while.24 = (s32[]{:T(128)}, f32[1,8,128]{2,1,0:T(8,128)S(1)}, f32[1,8,128]{2,1,0:T(8,128)S(1)}, f32[1,8,128,128]{3,2,1,0:T(8,128)S(1)}, f32[1,8,128]{2,1,0:T(8,...) while((s32[]{:T(128)}, f32[1,8,128]{2,1,0:T(8,128)S(1)}, ...), condition=%wide.region_9.10_spmd.clone, body=%wide.region_0.9_spmd.clone.sunk | while | flops 551165184 | bytes 16921084 | solution.py:114
  142.8 1.0 constant_dynamic-slice_fusion.5
  143.8 2.0 conditional.7
  145.9 2.0 conditional.6
  148.0 1.0 constant_dynamic-slice_fusion.5
  149.0 2.0 conditional.7
  151.1 2.0 conditional.6
  153.1 1.0 constant_dynamic-slice_fusion.5
  154.1 2.0 conditional.7
  156.2 2.0 conditional.6
  158.3 1.0 constant_dynamic-slice_fusion.5
  159.3 2.0 conditional.7
  161.4 2.0 conditional.6
  163.4 1.0 constant_dynamic-slice_fusion.5
  164.5 2.0 conditional.7
  166.5 2.0 conditional.6
  168.6 1.0 constant_dynamic-slice_fusion.5
  169.6 2.0 conditional.7
  171.7 2.0 conditional.6
  173.8 1.0 constant_dynamic-slice_fusion.5
  174.8 2.0 conditional.7
  176.8 2.0 conditional.6
  178.9 1.0 constant_dynamic-slice_fusion.5
  179.9 2.0 conditional.7
  182.0 2.0 conditional.6
  184.1 1.0 constant_dynamic-slice_fusion.5
  185.1 2.0 conditional.7
  187.1 2.0 conditional.6
  189.2 1.0 constant_dynamic-slice_fusion.5
  190.4 1.0 constant_dynamic-slice_fusion.5
  197.8 7.1 %convolution_convert_fusion = bf16[256,4096]{1,0:T(8,128)(2,1)} fusion(bf16[1024,4096]{1,0:T(8,128)(2,1)} %param.20, bf16[128,1024]{0,1:T(8,128)(2,1)S(1)} %bitcast.138, bf16[128,1024]{0,1:T(8,128)(2,1)S(1)} %bitcast.137), kind=kOutput, calls=%fused_computation.62 | convolution fusion | flops 2149580800 | bytes 11010048 | tf_op jit(solution)/shard_map/dot_general | solution.py:126
  206.4 102.8 %reduce-scatter.2.cloned.1.call-done = bf16[32,4096]{1,0:T(8,128)(2,1)} async-done(((bf16[256,4096]{1,0:T(8,128)(2,1)}), bf16[32,4096]{1,0:T(8,128)(2,1)}) %reduce-scatter.2.cloned.1.call-update) | async-done | bytes 262160 | tf_op jit(solution)/shard_map/reduce_scatter | solution.py:125
  309.2 1.1 fusion.55
  310.4 2.4 convolution_convert_fusion.2
  312.8 4.6 all-to-all-start
  317.6 22.4 %all-to-all-done = bf16[8,16,4096]{2,1,0:T(8,128)(2,1)S(1)} async-done(((bf16[8,16,4096]{2,1,0:T(8,128)(2,1)}), bf16[8,16,4096]{2,1,0:T(8,128)(2,1)S(1)}, u32[]{:S(2)}, u32[]{:S(2)}) %all-to-all-start) | async-done | bytes 1048608 | tf_op jit(solution)/shard_map/all_to_all | solution.py:153
  339.9 3.3 stack.3
  343.2 6.2 %all-to-all-start.1 = ((bf16[32,768,128]{1,2,0:T(8,128)(2,1)}), bf16[32,768,128]{1,2,0:T(8,128)(2,1)}, u32[]{:S(2)}, u32[]{:S(2)}) async-start(bf16[32,768,128]{1,2,0:T(8,128)(2,1)} %stack.3), calls=%async_computation.2 | async-start | bytes 12582912 | tf_op jit(solution)/shard_map/all_to_all | solution.py:16
  350.0 71.5 %all-gather.11.cloned.1.call-done = bf16[1,4096,768]{2,1,0:T(8,128)(2,1)} async-done(((bf16[1,128,768]{2,1,0:T(8,128)(2,1)}), bf16[1,4096,768]{2,1,0:T(8,128)(2,1)}) %all-gather.11.cloned.1.call-update) | async-done | bytes 6291472 | tf_op jit(solution)/shard_map/all_gather | solution.py:161
  421.5 3.8 fusion.44
  425.3 97.4 %all-to-all-done.1 = bf16[32,768,128]{1,2,0:T(8,128)(2,1)} async-done(((bf16[32,768,128]{1,2,0:T(8,128)(2,1)}), bf16[32,768,128]{1,2,0:T(8,128)(2,1)}, u32[]{:S(2)}, u32[]{:S(2)}) %all-to-all-start.1) | async-done | bytes 6291488 | tf_op jit(solution)/shard_map/all_to_all | solution.py:16
  522.7 21.8 %all-gather.13.cloned.1.call-done = bf16[1,4096,768]{2,1,0:T(8,128)(2,1)} async-done(((bf16[1,128,768]{2,1,0:T(8,128)(2,1)}), bf16[1,4096,768]{2,1,0:T(8,128)(2,1)}) %all-gather.13.cloned.1.call-update) | async-done | bytes 6291472 | tf_op jit(solution)/shard_map/all_gather | solution.py:166
  544.5 7.7 %convolution_convert_fusion.1 = bf16[128,4096]{1,0:T(8,128)(2,1)S(1)} fusion(bf16[768,4096]{0,1:T(8,128)(2,1)} %bitcast.37, bf16[128,4096]{1,0:T(8,128)(2,1)S(1)} %bitcast.128, bf16[1,4096,768]{2,1,0:T(8,128)(2,1)} %all-gather.13.cloned.1.call-done, f32[128,768]{1,0:T(8,128)S(1)} %fusion.44), kind=kOutput, calls=%fused_computation.63 | convolution fusion | flops 1611726848 | bytes 15073280 | tf_op jit(solution)/shard_map/dot_general | solution.py:171
  552.2 22.5 %all_to_all.15 = bf16[8,16,4096]{2,1,0:T(8,128)(2,1)S(1)} all-to-all(bf16[8,16,4096]{2,1,0:T(8,128)(2,1)S(1)} %bitcast.129), channel_id=1, replica_groups=mesh['ctx'=32,'exp'=8] {'exp'}, dimensions={0} | all-to-all | bytes 2097152 | tf_op jit(solution)/shard_map/all_to_all | solution.py:174
  (294 shorter events, 47.2 us)
Async XLA Ops:
  6.5 1.0 copy-start
  6.5 69.9 %all-gather.7.cloned.1.call-start = ((), (), s32[]{:S(2)}) async-start(), calls=%async_computation.4 | async-start | bytes 2162688 | tf_op jit(solution)/shard_map/all_gather | solution.py:89
  8.1 134.5 %all-gather.9.cloned.1.call-start = ((), (), s32[]{:S(2)}) async-start(), calls=%async_computation.5 | async-start | bytes 2162688 | tf_op jit(solution)/shard_map/all_gather | solution.py:90
  9.7 299.6 %reduce-scatter.2.cloned.1.call-start = ((), (), s32[]{:S(2)}) async-start(), calls=%async_computation.6 | async-start | bytes 2359296 | tf_op jit(solution)/shard_map/reduce_scatter | solution.py:125
  204.9 0.7 copy-start.5
  204.9 1.4 copy-start.4
  204.9 104.4 %copy-start.1 = (bf16[32,4096]{1,0:T(8,128)(2,1)S(1)}, bf16[32,4096]{1,0:T(8,128)(2,1)}, u32[]{:S(2)}) copy-start(bf16[32,4096]{1,0:T(8,128)(2,1)} %param.21) | copy-start | bytes 786436
  204.9 216.6 %all-gather.11.cloned.1.call-start = ((), (), s32[]{:S(2)}) async-start(), calls=%async_computation.7 | async-start | bytes 6488064 | tf_op jit(solution)/shard_map/all_gather | solution.py:161
  206.4 111.0 %copy-start.3 = (bf16[1,768,128]{2,1,0:T(8,128)(2,1)S(1)}, bf16[1,768,128]{2,1,0:T(8,128)(2,1)}, u32[]{:S(2)}) copy-start(bf16[1,768,128]{2,1,0:T(8,128)(2,1)} %param.27) | copy-start | bytes 589828
  312.8 27.1 %all-to-all-start = ((bf16[8,16,4096]{2,1,0:T(8,128)(2,1)}), bf16[8,16,4096]{2,1,0:T(8,128)(2,1)S(1)}, u32[]{:S(2)}, u32[]{:S(2)}) async-start(bf16[8,16,4096]{2,1,0:T(8,128)(2,1)} %bitcast.31), calls=%async_computation.1 | async-start | bytes 2097152 | tf_op jit(solution)/shard_map/all_to_all | solution.py:153
  343.2 179.4 %all-to-all-start.1 = ((bf16[32,768,128]{1,2,0:T(8,128)(2,1)}), bf16[32,768,128]{1,2,0:T(8,128)(2,1)}, u32[]{:S(2)}, u32[]{:S(2)}) async-start(bf16[32,768,128]{1,2,0:T(8,128)(2,1)} %stack.3), calls=%async_computation.2 | async-start | bytes 12582912 | tf_op jit(solution)/shard_map/all_to_all | solution.py:16
  349.4 195.1 %all-gather.13.cloned.1.call-start = ((), (), s32[]{:S(2)}) async-start(), calls=%async_computation.8 | async-start | bytes 6488064 | tf_op jit(solution)/shard_map/all_gather | solution.py:166
  552.2 22.5 %copy-start.6 = (f32[32,2]{0,1:T(2,128)S(1)}, f32[32,2]{0,1:T(2,128)}, u32[]{:S(2)}) copy-start(f32[32,2]{0,1:T(2,128)} %param.24) | copy-start | bytes 772
  552.2 22.8 %copy-start.2 = (bf16[32,4096]{1,0:T(8,128)(2,1)S(1)}, bf16[32,4096]{1,0:T(8,128)(2,1)}, u32[]{:S(2)}) copy-start(bf16[32,4096]{1,0:T(8,128)(2,1)} %reduce-scatter.2.cloned.1.call-done) | copy-start | bytes 786436
Sparse Core Ops, SparseCore 0:
  9.2 67.1 all-gather.6
  78.3 64.3 all-gather.8
  205.0 104.1 reduce-scatter.1
  311.0 110.4 all-gather.10
  423.2 121.2 all-gather.12
